TPU v7x, 32 devices: a whole 2x2x4 slice. The times are simulated.
32 devices in a mesh: seq: 16 (over z, x, core), wshard: 2 (over y).
Axes of the slice: x: 2, y: 2, z: 4, core: 2. Of those that a mesh axis runs over, the one named last changes fastest.
Arguments:
- block_input: float32 [2, 2048, 640], P('wshard', 'seq'), may hold values from -36 to 36
- attn_in: bfloat16 [640, 1536], P('wshard', 'seq'), may hold values from -0.25 to 0.25
- attn_out: bfloat16 [1024, 640], P('wshard', 'seq'), may hold values from -0.1875 to 0.1875
- ffn_in: bfloat16 [640, 4096], P('wshard', 'seq'), may hold values from -0.25 to 0.25
- ffn_out: bfloat16 [2048, 640], P('wshard', 'seq'), may hold values from -0.125 to 0.125
- norm_gains: bfloat16 [4, 640], P('wshard', 'seq'), may hold values from 0.25 to 1.75
- head_gains: bfloat16 [2, 256], P('wshard', 'seq'), may hold values from 0.25 to 1.75
- cotangent: float32 [2, 2048, 640], P('wshard', 'seq'), may hold values from -6 to 6
Outputs:
- block_output: float32 [2, 2048, 640], P('wshard', 'seq')
- input_grad: float32 [2, 2048, 640], P('wshard', 'seq')
- grad_attnin: float32 [640, 1536], P('wshard', 'seq')
- grad_attnout: float32 [1024, 640], P('wshard', 'seq')
- grad_ffnin: float32 [640, 4096], P('wshard', 'seq')
- grad_ffnout: float32 [2048, 640], P('wshard', 'seq')
- grad_norms: float32 [4, 640], P('wshard', 'seq')
- grad_heads: float32 [2, 256], P('wshard', 'seq')
All inputs are finite; a program needn't handle non-finite values.
Results may differ from a plain program's by a relative error of at most 0.02.
Values may be sent and summed in bfloat16 or wider, within the bound.
A program may use at most 128 MiB of HBM per device.

v0:
```python
import math

import jax
import jax.numpy as jnp
from jax import lax
from jax.sharding import PartitionSpec as P

NQ = 4
HD = 256
FF = 2048
WIN = 512


EPS = 1e-06
QUERY_SCALE = 0.0625


def shifted(value, axis, steps):
    count = lax.axis_size(axis)
    initial, last = (max(0, -steps), min(count, count - steps))
    return lax.ppermute(value, axis, [(source, source + steps) for source in range(initial, last)])


def rms_forward(values, gain_row):
    inverse_rms = lax.rsqrt(jnp.mean(values * values, axis=-1, keepdims=True) + EPS)
    normed = values * inverse_rms
    return (normed * gain_row, normed, inverse_rms)


def rms_backward(normed, inverse_rms, gain_row, upstream):
    scaled = upstream * gain_row
    through = inverse_rms * (scaled - normed * jnp.mean(scaled * normed, axis=-1, keepdims=True))
    return (through, upstream * normed)


def rotary_tables(positions, head_size):
    half_size = head_size // 2
    inverse_freq = jnp.exp(
        jnp.arange(half_size, dtype=jnp.float32) * (-2.0 * math.log(10000.0) / head_size)
    )
    angles = positions.astype(jnp.float32)[:, None] * inverse_freq[None, :]
    return (jnp.cos(angles), jnp.sin(angles))


def rotate(values, cosine_table, sine_table):
    half_size = values.shape[-1] // 2
    first_half = values[..., :half_size]
    second_half = values[..., half_size:]
    cosine_row = cosine_table[:, None, :]
    sine_row = sine_table[:, None, :]
    return jnp.concatenate(
        [
            first_half * cosine_row - second_half * sine_row,
            second_half * cosine_row + first_half * sine_row,
        ],
        axis=-1,
    )


def gated_gelu(gate_part, up_part):
    return jax.nn.gelu(gate_part, approximate=True) * up_part


def window_mask(query_positions, key_positions):
    query_column = query_positions[:, None]
    key_line = key_positions[None, :]
    return (key_line >= 0) & (key_line <= query_column) & (key_line > query_column - WIN)


def attend(query_block, key_block, value_block, allowed):
    scores = jnp.dot(query_block, key_block.T, preferred_element_type=jnp.float32)
    exponent = jnp.where(allowed, jnp.exp(scores), 0.0)
    totals = jnp.sum(exponent, axis=-1, keepdims=True)
    probabilities = (exponent / totals).astype(jnp.bfloat16)
    mixture = jnp.dot(probabilities, value_block, preferred_element_type=jnp.float32).astype(
        jnp.bfloat16
    )
    return (mixture, jnp.log(totals))


def attend_back(query_block, key_block, value_block, allowed, mixture, log_totals, d_mixture):
    scores = jnp.dot(query_block, key_block.T, preferred_element_type=jnp.float32)
    probabilities = jnp.where(allowed, jnp.exp(scores - log_totals), 0.0)
    delta_row = jnp.sum(
        d_mixture.astype(jnp.float32) * mixture.astype(jnp.float32), axis=-1, keepdims=True
    )
    d_probs = jnp.dot(d_mixture, value_block.T, preferred_element_type=jnp.float32)
    d_scores = (probabilities * (d_probs - delta_row)).astype(jnp.bfloat16)
    d_values = jnp.dot(
        probabilities.astype(jnp.bfloat16).T, d_mixture, preferred_element_type=jnp.float32
    )
    d_queries = jnp.dot(d_scores, key_block, preferred_element_type=jnp.float32)
    d_keys = jnp.dot(d_scores.T, query_block, preferred_element_type=jnp.float32)
    return (d_queries, d_keys, d_values)


def shards(block_input, attn_in, attn_out, ffn_in, ffn_out, norm_gains, head_gains, cotangent):
    paired = (
        lax.all_gather(attn_in, "wshard", axis=0, tiled=True),
        lax.all_gather(attn_out, "wshard", axis=0, tiled=True),
        lax.all_gather(ffn_in, "wshard", axis=0, tiled=True),
        lax.all_gather(ffn_out, "wshard", axis=0, tiled=True),
        lax.all_gather(norm_gains, "wshard", axis=0, tiled=True),
        lax.all_gather(head_gains, "wshard", axis=0, tiled=True),
    )
    whole = (
        lax.all_gather(paired[0], "seq", axis=1, tiled=True),
        lax.all_gather(paired[1], "seq", axis=1, tiled=True),
        lax.all_gather(paired[2], "seq", axis=1, tiled=True),
        lax.all_gather(paired[3], "seq", axis=1, tiled=True),
        lax.all_gather(paired[4], "seq", axis=1, tiled=True),
        lax.all_gather(paired[5], "seq", axis=1, tiled=True),
    )
    whole_attnin, whole_attnout, whole_ffnin, whole_ffnout, whole_norms, whole_heads = whole
    gain_table = whole_norms.astype(jnp.float32)
    head_table = whole_heads.astype(jnp.float32)
    tokens = block_input[0]
    upstream_out = cotangent[0]
    row_count = tokens.shape[0]
    hop_count = (WIN - 1) // row_count + 1
    positions = lax.axis_index("seq") * row_count + jnp.arange(row_count, dtype=jnp.int32)
    normed_in, unit_in, inverse_in = rms_forward(tokens, gain_table[0])
    hidden_in = normed_in.astype(jnp.bfloat16)
    projected = jnp.dot(hidden_in, whole_attnin, preferred_element_type=jnp.float32)
    query_raw = projected[:, : NQ * HD].reshape(row_count, NQ, HD)
    key_raw = projected[:, NQ * HD : (NQ + 1) * HD].reshape(row_count, 1, HD)
    value_raw = projected[:, (NQ + 1) * HD :]
    query_norm, query_unit, query_inverse = rms_forward(query_raw, head_table[0])
    key_norm, key_unit, key_inverse = rms_forward(key_raw, head_table[1])
    cosine_table, sine_table = rotary_tables(positions, HD)
    query_rot = (
        (rotate(query_norm, cosine_table, sine_table) * QUERY_SCALE)
        .astype(jnp.bfloat16)
        .reshape(row_count * NQ, HD)
    )
    key_rot = rotate(key_norm, cosine_table, sine_table).reshape(row_count, HD).astype(jnp.bfloat16)
    own_pair = jnp.concatenate([key_rot, value_raw.astype(jnp.bfloat16)], axis=1)
    earlier = []
    for distance in range(hop_count, 0, -1):
        earlier.append(shifted(own_pair, "seq", distance))
    window_pair = jnp.concatenate(earlier + [own_pair], axis=0)
    keys_all = window_pair[:, :HD]
    values_all = window_pair[:, HD:]
    key_positions = (
        positions[0]
        - hop_count * row_count
        + jnp.arange((hop_count + 1) * row_count, dtype=jnp.int32)
    )
    allowed = window_mask(jnp.repeat(positions, NQ), key_positions)
    mixture, log_totals = attend(query_rot, keys_all, values_all, allowed)
    attended = mixture.reshape(row_count, NQ * HD)
    attn_proj = jnp.dot(attended, whole_attnout, preferred_element_type=jnp.float32)
    post_attn, unit_attn, inverse_attn = rms_forward(attn_proj, gain_table[1])
    middle = tokens + post_attn
    normed_mid, unit_mid, inverse_mid = rms_forward(middle, gain_table[2])
    hidden_mid = normed_mid.astype(jnp.bfloat16)
    gate_up = jnp.dot(hidden_mid, whole_ffnin, preferred_element_type=jnp.float32)
    activated, gelu_back = jax.vjp(gated_gelu, gate_up[:, :FF], gate_up[:, FF:])
    activated_bf = activated.astype(jnp.bfloat16)
    ffn_proj = jnp.dot(activated_bf, whole_ffnout, preferred_element_type=jnp.float32)
    post_ffn, unit_ffn, inverse_ffn = rms_forward(ffn_proj, gain_table[3])
    output = middle + post_ffn
    d_ffnproj, gain_four = rms_backward(unit_ffn, inverse_ffn, gain_table[3], upstream_out)
    d_ffn_bf = d_ffnproj.astype(jnp.bfloat16)
    grad_ffnout = jnp.dot(activated_bf.T, d_ffn_bf, preferred_element_type=jnp.float32)
    d_activated = jnp.dot(d_ffn_bf, whole_ffnout.T, preferred_element_type=jnp.float32)
    d_gate, d_up = gelu_back(d_activated)
    d_gateup = jnp.concatenate([d_gate, d_up], axis=1).astype(jnp.bfloat16)
    grad_ffnin = jnp.dot(hidden_mid.T, d_gateup, preferred_element_type=jnp.float32)
    d_normmid = jnp.dot(d_gateup, whole_ffnin.T, preferred_element_type=jnp.float32)
    d_middle_part, gain_three = rms_backward(unit_mid, inverse_mid, gain_table[2], d_normmid)
    d_middle = upstream_out + d_middle_part
    d_attnproj, gain_two = rms_backward(unit_attn, inverse_attn, gain_table[1], d_middle)
    d_attn_bf = d_attnproj.astype(jnp.bfloat16)
    grad_attnout = jnp.dot(attended.T, d_attn_bf, preferred_element_type=jnp.float32)
    d_mixed = jnp.dot(d_attn_bf, whole_attnout.T, preferred_element_type=jnp.float32).astype(
        jnp.bfloat16
    )
    d_mixed = d_mixed.reshape(row_count * NQ, HD)
    d_queries, d_keys, d_values = attend_back(
        query_rot, keys_all, values_all, allowed, mixture, log_totals, d_mixed
    )
    pair_all = jnp.concatenate([d_keys, d_values], axis=1)
    pair_grad = pair_all[hop_count * row_count :]
    for distance in range(1, hop_count + 1):
        start_row = (hop_count - distance) * row_count
        pair_grad = pair_grad + shifted(
            pair_all[start_row : start_row + row_count].astype(jnp.bfloat16), "seq", -distance
        ).astype(jnp.float32)
    d_keynorm = rotate(pair_grad[:, :HD].reshape(row_count, 1, HD), cosine_table, -sine_table)
    d_keyraw, gain_key = rms_backward(key_unit, key_inverse, head_table[1], d_keynorm)
    d_queryrot = d_queries.reshape(row_count, NQ, HD) * QUERY_SCALE
    d_querynorm = rotate(d_queryrot, cosine_table, -sine_table)
    d_queryraw, gain_query = rms_backward(query_unit, query_inverse, head_table[0], d_querynorm)
    d_projected = jnp.concatenate(
        [
            d_queryraw.reshape(row_count, NQ * HD),
            d_keyraw.reshape(row_count, HD),
            pair_grad[:, HD:],
        ],
        axis=1,
    ).astype(jnp.bfloat16)
    grad_attnin = jnp.dot(hidden_in.T, d_projected, preferred_element_type=jnp.float32)
    d_normin = jnp.dot(d_projected, whole_attnin.T, preferred_element_type=jnp.float32)
    d_tokens_part, gain_one = rms_backward(unit_in, inverse_in, gain_table[0], d_normin)
    input_grad = d_middle + d_tokens_part
    grad_norms = jnp.stack(
        [
            jnp.sum(gain_one, axis=0),
            jnp.sum(gain_two, axis=0),
            jnp.sum(gain_three, axis=0),
            jnp.sum(gain_four, axis=0),
        ]
    )
    grad_heads = jnp.stack(
        [jnp.sum(gain_query.reshape(-1, HD), axis=0), jnp.sum(gain_key.reshape(-1, HD), axis=0)]
    )
    partial_sums = (
        lax.psum_scatter(grad_attnin, "seq", scatter_dimension=1, tiled=True),
        lax.psum_scatter(grad_attnout, "seq", scatter_dimension=1, tiled=True),
        lax.psum_scatter(grad_ffnin, "seq", scatter_dimension=1, tiled=True),
        lax.psum_scatter(grad_ffnout, "seq", scatter_dimension=1, tiled=True),
        lax.psum_scatter(grad_norms, "seq", scatter_dimension=1, tiled=True),
        lax.psum_scatter(grad_heads, "seq", scatter_dimension=1, tiled=True),
    )
    reduced = (
        lax.psum_scatter(
            partial_sums[0].astype(jnp.bfloat16), "wshard", scatter_dimension=0, tiled=True
        ).astype(jnp.float32),
        lax.psum_scatter(
            partial_sums[1].astype(jnp.bfloat16), "wshard", scatter_dimension=0, tiled=True
        ).astype(jnp.float32),
        lax.psum_scatter(
            partial_sums[2].astype(jnp.bfloat16), "wshard", scatter_dimension=0, tiled=True
        ).astype(jnp.float32),
        lax.psum_scatter(
            partial_sums[3].astype(jnp.bfloat16), "wshard", scatter_dimension=0, tiled=True
        ).astype(jnp.float32),
        lax.psum_scatter(
            partial_sums[4].astype(jnp.bfloat16), "wshard", scatter_dimension=0, tiled=True
        ).astype(jnp.float32),
        lax.psum_scatter(
            partial_sums[5].astype(jnp.bfloat16), "wshard", scatter_dimension=0, tiled=True
        ).astype(jnp.float32),
    )
    return (
        output[None],
        input_grad[None],
        reduced[0],
        reduced[1],
        reduced[2],
        reduced[3],
        reduced[4],
        reduced[5],
    )


def solution(mesh):
    in_specs = (
        P("wshard", "seq", None),
        P("wshard", "seq"),
        P("wshard", "seq"),
        P("wshard", "seq"),
        P("wshard", "seq"),
        P("wshard", "seq"),
        P("wshard", "seq"),
        P("wshard", "seq", None),
    )
    out_specs = (
        P("wshard", "seq", None),
        P("wshard", "seq", None),
        P("wshard", "seq"),
        P("wshard", "seq"),
        P("wshard", "seq"),
        P("wshard", "seq"),
        P("wshard", "seq"),
        P("wshard", "seq"),
    )
    return jax.shard_map(shards, mesh=mesh, in_specs=in_specs, out_specs=out_specs, check_vma=False)
```

profile of v0, /device:TPU:0, one launch (start us, length us, event | category | flops | bytes accessed | tf_op | source)
XLA Modules:
  0.0 676.5 jit_solution(15655471984037056477)
XLA Ops:
  7.2 6.4 all-gather.2
  14.6 6.3 all_gather.42
  21.0 6.5 all_gather.44
  27.6 5.2 all_gather.46
  33.1 4.2 all-gather
  37.3 21.8 %all-gather.1 = bf16[16,40,4]{1,2,0:T(4,128)(2,1)S(1)} all-gather(bf16[1,40,4]{1,2,0:T(4,128)(2,1)S(1)} %bitcast.139), channel_id=1, replica_groups=mesh['seq'=16,'wshard'=2] {'seq'}, dimensions={0}, use_global_device_ids=true | all-gather | bytes 5440 | tf_op jit(solution)/shard_map/all_gather | solution.py:111
  59.7 4.2 all-gather.3
  63.9 17.1 %all-gather.4 = bf16[16,16,2]{1,2,0:T(2,128)(2,1)S(1)} all-gather(bf16[1,16,2]{1,2,0:T(2,128)(2,1)S(1)} %bitcast.141), channel_id=1, replica_groups=mesh['seq'=16,'wshard'=2] {'seq'}, dimensions={0}, use_global_device_ids=true | all-gather | bytes 1088 | tf_op jit(solution)/shard_map/all_gather | solution.py:112
  87.0 3.9 collective-permute-start.1
  103.8 54.8 %all-gather.14.cloned.1.call-done = bf16[640,4096]{1,0:T(8,128)(2,1)} async-done(((bf16[640,256]{1,0:T(8,128)(2,1)}), bf16[640,4096]{1,0:T(8,128)(2,1)}) %all-gather.14.cloned.1.call-update) | async-done | bytes 5242896 | tf_op jit(solution)/shard_map/all_gather | solution.py:109
  158.6 3.5 fusion.69
  163.3 38.7 %all-gather.16.cloned.1.call-done = bf16[2048,640]{0,1:T(8,128)(2,1)} async-done(((bf16[2048,40]{0,1:T(8,128)(2,1)}), bf16[2048,640]{0,1:T(8,128)(2,1)}) %all-gather.16.cloned.1.call-update) | async-done | bytes 2621456 | tf_op jit(solution)/shard_map/all_gather | solution.py:110
  243.3 5.7 fusion.12
  251.4 27.1 %reduce-scatter.17.cloned.1.call-done = f32[1024,40]{0,1:T(8,128)} async-done(((f32[1024,640]{0,1:T(8,128)}), f32[1024,40]{0,1:T(8,128)}) %reduce-scatter.17.cloned.1.call-update) | async-done | bytes 163856 | tf_op jit(solution)/shard_map/reduce_scatter | solution.py:220
  280.1 71.6 %reduce-scatter.15.cloned.1.call-done = f32[640,96]{0,1:T(8,128)} async-done(((f32[640,1536]{0,1:T(8,128)}), f32[640,96]{0,1:T(8,128)}) %reduce-scatter.15.cloned.1.call-update) | async-done | bytes 245776 | tf_op jit(solution)/shard_map/reduce_scatter | solution.py:219
  356.1 76.8 %reduce-scatter.25.cloned.1.call-done = f32[2048,40]{0,1:T(8,128)} async-done(((f32[2048,640]{0,1:T(8,128)}), f32[2048,40]{0,1:T(8,128)}) %reduce-scatter.25.cloned.1.call-update) | async-done | bytes 327696 | tf_op jit(solution)/shard_map/reduce_scatter | solution.py:222
  435.3 60.0 %all-reduce = bf16[4,640]{1,0:T(4,128)(2,1)S(1)} all-reduce(f32[4,640]{1,0:T(4,128)S(1)} %pad_maximum_fusion.10), channel_id=10, replica_groups=mesh['seq'=16,'wshard'=2] {'seq'}, use_global_device_ids=true, to_apply=%region_26.27.clone | all-reduce | flops 2560 | bytes 15360
  495.4 60.2 %reduce-scatter.21.cloned.1.call-done = f32[640,256]{1,0:T(8,128)} async-done(((f32[640,4096]{1,0:T(8,128)}), f32[640,256]{1,0:T(8,128)}) %reduce-scatter.21.cloned.1.call-update) | async-done | bytes 655376 | tf_op jit(solution)/shard_map/reduce_scatter | solution.py:221
  558.4 56.6 %reduce-scatter.31.cloned.1.call-done = f32[16,2]{1,0:T(8,128)} async-done(((f32[256,2]{1,0:T(8,128)}), f32[16,2]{1,0:T(8,128)}) %reduce-scatter.31.cloned.1.call-update) | async-done | bytes 144
  615.7 4.9 all-reduce.3
  622.3 4.3 reduce-scatter.19.cloned.1.call-done
  628.1 12.1 %reduce-scatter.29.cloned.1.call-done = bf16[320,96]{1,0:T(8,128)(2,1)} async-done(((bf16[640,96]{1,0:T(8,128)(2,1)}), bf16[320,96]{1,0:T(8,128)(2,1)}) %reduce-scatter.29.cloned.1.call-update) | async-done | bytes 61456
  641.9 11.1 %reduce-scatter.27.cloned.1.call-done = bf16[1024,40]{0,1:T(8,128)(2,1)} async-done(((bf16[2048,40]{0,1:T(8,128)(2,1)}), bf16[1024,40]{0,1:T(8,128)(2,1)}) %reduce-scatter.27.cloned.1.call-update) | async-done | bytes 81936 | tf_op jit(solution)/shard_map/reduce_scatter | solution.py:236
  654.5 13.8 %reduce-scatter.23.cloned.1.call-done = bf16[320,256]{1,0:T(8,128)(2,1)} async-done(((bf16[640,256]{1,0:T(8,128)(2,1)}), bf16[320,256]{1,0:T(8,128)(2,1)}) %reduce-scatter.23.cloned.1.call-update) | async-done | bytes 163856 | tf_op jit(solution)/shard_map/reduce_scatter | solution.py:233
  (311 shorter events, 82.9 us)
Async XLA Ops:
  7.2 75.5 %all-gather.10.cloned.1.call-start = ((), (), s32[]{:S(2)}) async-start(), calls=%async_computation.9 | async-start | bytes 2088960 | tf_op jit(solution)/shard_map/all_gather | solution.py:107
  14.6 85.8 %all-gather.12.cloned.1.call-start = ((), (), s32[]{:S(2)}) async-start(), calls=%async_computation.10 | async-start | bytes 1392640 | tf_op jit(solution)/shard_map/all_gather | solution.py:108
  21.0 137.7 %all-gather.14.cloned.1.call-start = ((), (), s32[]{:S(2)}) async-start(), calls=%async_computation.11 | async-start | bytes 5570560 | tf_op jit(solution)/shard_map/all_gather | solution.py:109
  27.6 174.5 %all-gather.16.cloned.1.call-start = ((), (), s32[]{:S(2)}) async-start(), calls=%async_computation.12 | async-start | bytes 2785280 | tf_op jit(solution)/shard_map/all_gather | solution.py:110
  32.9 245.6 %reduce-scatter.17.cloned.1.call-start = ((), (), s32[]{:S(2)}) async-start(), calls=%async_computation.14 | async-start | bytes 2785280 | tf_op jit(solution)/shard_map/reduce_scatter | solution.py:220
  85.7 11.5 %collective-permute-start = (bf16[128,512]{1,0:T(8,128)(2,1)S(1)}, bf16[128,512]{1,0:T(8,128)(2,1)S(1)}, u32[]{:S(2)}, u32[]{:S(2)}) collective-permute-start(bf16[128,512]{1,0:T(8,128)(2,1)S(1)} %pad_maximum_fusion.8), channel_id=1, source_target_pairs={{0,8},{2,10},{4,12},{6,14},{8,16},{10,18},{12,20},{14,22},{16,24},... | collective-permute-start | bytes 393224 | tf_op jit(solution)/shard_map/ppermute | solution.py:21
  87.0 10.2 %collective-permute-start.1 = (bf16[128,512]{1,0:T(8,128)(2,1)S(1)}, bf16[128,512]{1,0:T(8,128)(2,1)S(1)}, u32[]{:S(2)}, u32[]{:S(2)}) collective-permute-start(bf16[128,512]{1,0:T(8,128)(2,1)S(1)} %pad_maximum_fusion.8), channel_id=1, source_target_pairs={{0,6},{2,8},{4,10},{6,12},{8,14},{10,16},{12,18},{14,20},{16,22},{... | collective-permute-start | bytes 393224 | tf_op jit(solution)/shard_map/ppermute | solution.py:21
  90.8 6.4 collective-permute-start.2
  92.2 5.1 collective-permute-start.3
  215.3 136.4 %reduce-scatter.15.cloned.1.call-start = ((), (), s32[]{:S(2)}) async-start(), calls=%async_computation.13 | async-start | bytes 4177920 | tf_op jit(solution)/shard_map/reduce_scatter | solution.py:219
  221.1 12.0 %collective-permute-start.7 = (bf16[128,512]{1,0:T(8,128)(2,1)}, bf16[128,512]{1,0:T(8,128)(2,1)}, u32[]{:S(2)}, u32[]{:S(2)}) collective-permute-start(bf16[128,512]{1,0:T(8,128)(2,1)} %get-tuple-element.32), channel_id=1, source_target_pairs={{8,0},{10,2},{12,4},{14,6},{16,8},{18,10},{20,12},{22,14},{24,16},... | collective-permute-start | bytes 393224 | tf_op jit(solution)/shard_map/ppermute | solution.py:21
  222.6 10.6 %collective-permute-start.6 = (bf16[128,512]{1,0:T(8,128)(2,1)}, bf16[128,512]{1,0:T(8,128)(2,1)}, u32[]{:S(2)}, u32[]{:S(2)}) collective-permute-start(bf16[128,512]{1,0:T(8,128)(2,1)} %get-tuple-element.33), channel_id=1, source_target_pairs={{6,0},{8,2},{10,4},{12,6},{14,8},{16,10},{18,12},{20,14},{22,16},{... | collective-permute-start | bytes 393224 | tf_op jit(solution)/shard_map/ppermute | solution.py:21
  223.9 9.3 %collective-permute-start.5 = (bf16[128,512]{1,0:T(8,128)(2,1)}, bf16[128,512]{1,0:T(8,128)(2,1)}, u32[]{:S(2)}, u32[]{:S(2)}) collective-permute-start(bf16[128,512]{1,0:T(8,128)(2,1)} %get-tuple-element.34), channel_id=1, source_target_pairs={{4,0},{6,2},{8,4},{10,6},{12,8},{14,10},{16,12},{18,14},{20,16},{2... | collective-permute-start | bytes 393224 | tf_op jit(solution)/shard_map/ppermute | solution.py:21
  225.4 7.8 %collective-permute-start.4 = (bf16[128,512]{1,0:T(8,128)(2,1)}, bf16[128,512]{1,0:T(8,128)(2,1)}, u32[]{:S(2)}, u32[]{:S(2)}) collective-permute-start(bf16[128,512]{1,0:T(8,128)(2,1)} %get-tuple-element.31), channel_id=1, source_target_pairs={{2,0},{4,2},{6,4},{8,6},{10,8},{12,10},{14,12},{16,14},{18,16},{20... | collective-permute-start | bytes 393224 | tf_op jit(solution)/shard_map/ppermute | solution.py:21
  237.8 195.1 %reduce-scatter.25.cloned.1.call-start = ((), (), s32[]{:S(2)}) async-start(), calls=%async_computation.18 | async-start | bytes 5570560 | tf_op jit(solution)/shard_map/reduce_scatter | solution.py:222
  242.1 313.5 %reduce-scatter.21.cloned.1.call-start = ((), (), s32[]{:S(2)}) async-start(), calls=%async_computation.16 | async-start | bytes 11141120 | tf_op jit(solution)/shard_map/reduce_scatter | solution.py:221
  249.0 366.0 %reduce-scatter.31.cloned.1.call-start = ((), (), s32[]{:S(2)}) async-start(), calls=%async_computation.21 | async-start | bytes 139264
  250.3 184.4 %copy-start.16 = (bf16[128,1024]{1,0:T(8,128)(2,1)S(1)}, bf16[128,1024]{1,0:T(8,128)(2,1)}, u32[]{:S(2)}) copy-start(bf16[128,1024]{1,0:T(8,128)(2,1)} %copy-done.15) | copy-start | bytes 786436
  250.4 184.2 %copy-start.12 = (bf16[640,1536]{0,1:T(8,128)(2,1)S(1)}, bf16[640,1536]{0,1:T(8,128)(2,1)}, u32[]{:S(2)}) copy-start(bf16[640,1536]{0,1:T(8,128)(2,1)} %all-gather.10.cloned.1.call-done) | copy-start | bytes 5898244
  250.5 184.2 %copy-start.48 = (f32[128]{0:T(128)S(1)}, f32[128]{0:T(128)}, u32[]{:S(2)}) copy-start(f32[128]{0:T(128)} %copy-done.46) | copy-start | bytes 1540
  251.3 375.4 %reduce-scatter.19.cloned.1.call-start = ((), (), s32[]{:S(2)}) async-start(), calls=%async_computation.15 | async-start | bytes 122880 | tf_op jit(solution)/shard_map/reduce_scatter | solution.py:230
  280.0 360.2 %reduce-scatter.29.cloned.1.call-start = ((), (), s32[]{:S(2)}) async-start(), calls=%async_computation.20 | async-start | bytes 245760
  353.5 299.5 %reduce-scatter.27.cloned.1.call-start = ((), (), s32[]{:S(2)}) async-start(), calls=%async_computation.19 | async-start | bytes 245760 | tf_op jit(solution)/shard_map/reduce_scatter | solution.py:236
  434.6 233.7 %reduce-scatter.23.cloned.1.call-start = ((), (), s32[]{:S(2)}) async-start(), calls=%async_computation.17 | async-start | bytes 491520 | tf_op jit(solution)/shard_map/reduce_scatter | solution.py:233
  (70 other events, 1151.7 us)
Sparse Core Ops, SparseCore 0:
  14.7 42.8 all-gather.9
  59.9 37.4 all-gather.11
  99.5 59.0 all-gather.13
  160.7 41.2 all-gather.15
  215.4 63.0 reduce-scatter.16
  282.2 69.4 reduce-scatter.14
  355.6 77.3 reduce-scatter.24
  437.0 118.5 reduce-scatter.20
  559.7 55.2 reduce-scatter.30
  617.5 9.1 reduce-scatter.18
  629.5 10.6 reduce-scatter.28
  642.3 10.6 reduce-scatter.26
  655.8 12.4 reduce-scatter.22
where the time goes:
time: 678 us; the launch traced here: 676 us
  waiting for transfers between devices  427 us (63%)
  blocking collectives  137 us (20%)
  matrix products  35 us (5%)
  other arithmetic  24.6 us (4%)
  local copies, waits for them, and re-layouts  20.7 us (3%)
  between operations  16.6 us (2%)
  starting transfers between devices  15.3 us (2%)
    reduce_scatter x1, waiting for transfers between devices, shards(): lax.psum_scatter(grad_ffnout, 'seq', scatter_dimension=1, tiled=True)  76.8 us
    reduce_scatter x1, waiting for transfers between devices, shards(): lax.psum_scatter(grad_attnin, 'seq', scatter_dimension=1, tiled=True)  71.6 us
    unnamed x15, waiting for transfers between devices  68.9 us
    unnamed x2, blocking collectives  64.9 us
    reduce_scatter x1, waiting for transfers between devices, shards(): lax.psum_scatter(grad_ffnin, 'seq', scatter_dimension=1, tiled=True)  60.2 us
    all_gather x1, waiting for transfers between devices, shards(): lax.all_gather(paired[2], 'seq', axis=1, tiled=True)  54.8 us
    all_gather x1, waiting for transfers between devices, shards(): lax.all_gather(paired[3], 'seq', axis=1, tiled=True)  38.7 us
    reduce_scatter x1, waiting for transfers between devices, shards(): lax.psum_scatter(grad_attnout, 'seq', scatter_dimension=1, tiled=True)  27.1 us
  transfers between devices with their start and end apart: 21, of which 11 were waited for; matrix products, arithmetic and copies ran while one was open for 9% of the time, Pallas kernels for 0%

commit v1 on v0

--- a/solution.py
+++ b/solution.py
@@ -3,6 +3,8 @@
 import jax
 import jax.numpy as jnp
 from jax import lax
+from jax.experimental import pallas as pl
+from jax.experimental.pallas import tpu as pltpu
 from jax.sharding import PartitionSpec as P
 
 NQ = 4
@@ -94,24 +96,292 @@
     return (d_queries, d_keys, d_values)
 
 
+MESH = pl.DeviceIdType.MESH
+
+
+def axis_bits(count):
+    return count.bit_length() - 1
+
+
+def coordinates(bits):
+    place = lax.axis_index("seq")
+    values = [lax.axis_index("wshard")]
+    for bit in range(bits - 1, -1, -1):
+        values.append(lax.rem(lax.div(place, 2**bit), 2))
+    return values
+
+
+def partner(dim, coords, bits):
+    if dim == 0:
+        return (lax.axis_index("seq"), 1 - coords[0])
+    step = 2 ** (bits - dim)
+    return (lax.axis_index("seq") + (1 - 2 * coords[dim]) * step, lax.axis_index("wshard"))
+
+
+def greet(coords, bits):
+    barrier = pltpu.get_barrier_semaphore()
+    for dim in range(bits + 1):
+        pl.semaphore_signal(
+            barrier, inc=1, device_id=partner(dim, coords, bits), device_id_type=MESH
+        )
+    pl.semaphore_wait(barrier, bits + 1)
+
+
+def scatter_order(bits, flipped):
+    middle = [0, bits - 1] if flipped else [bits - 1, 0]
+    return [bits] + middle + list(range(bits - 2, 0, -1))
+
+
+class Piece:
+    def __init__(self, ref, rows, lanes, wdim, lane_part, flipped, dtype=jnp.bfloat16):
+        self.ref, self.rows, self.lanes, self.wdim = ref, rows, lanes, wdim
+        self.lane_part, self.flipped, self.dtype = lane_part, flipped, dtype
+
+    def slices(self, picks, bits, base_lane):
+        index = []
+        rows, lanes = pl.ds(0, self.rows), pl.ds(base_lane, self.lanes)
+        if 0 in picks:
+            pick = picks[0]
+            if self.wdim == "lead":
+                index.append(slice(None) if pick is None else pick)
+            elif self.wdim == "rows":
+                if pick is None:
+                    rows = pl.ds(0, 2 * self.rows)
+                else:
+                    rows = pl.ds(pl.multiple_of(pick * self.rows, self.rows), self.rows)
+            else:
+                if pick is None:
+                    lanes = pl.ds(0, 2 * self.lanes)
+                else:
+                    lanes = pl.ds(pl.multiple_of(pick * self.lanes, self.lanes), self.lanes)
+        for dim in range(1, bits + 1):
+            if dim in picks:
+                pick = picks[dim]
+                index.append(slice(None) if pick is None else pick)
+        return tuple(index) + (rows, lanes)
+
+    def shape(self, dims):
+        rows, lanes, lead = self.rows, self.lanes, []
+        for dim in sorted(dims):
+            if dim > 0 or self.wdim == "lead":
+                lead.append(2)
+            elif self.wdim == "rows":
+                rows *= 2
+            else:
+                lanes *= 2
+        return tuple(lead) + (rows, lanes)
+
+
+def gather_pieces(shapes):
+    out = []
+    for number, (rows, lanes, wdim, parts) in enumerate(shapes):
+        for part in range(parts):
+            out.append(
+                Piece(number, rows, lanes // parts, wdim, part, (part == 1) or (number % 2 == 1))
+            )
+    return out
+
+
+def gather_kernel(pieces, bits, count, *refs):
+    blocks, outs = refs[:count], refs[count : 2 * count]
+    send_sems, recv_sems, local_sems = refs[2 * count :]
+    coords = coordinates(bits)
+    own = {dim: coords[dim] for dim in range(bits + 1)}
+    local = []
+    for number, piece in enumerate(pieces):
+        lane = piece.lane_part * piece.lanes
+        copy = pltpu.make_async_copy(
+            blocks[piece.ref].at[:, pl.ds(lane, piece.lanes)],
+            outs[piece.ref].at[piece.slices(own, bits, lane)],
+            local_sems.at[number],
+        )
+        copy.start()
+        local.append(copy)
+    greet(coords, bits)
+    orders = [scatter_order(bits, piece.flipped)[::-1] for piece in pieces]
+    held = [dict(own) for _ in pieces]
+    last = list(local)
+    sent = []
+    for stage in range(bits + 1):
+        for number, piece in enumerate(pieces):
+            if stage == 0:
+                last[number].wait()
+            else:
+                last[number].wait_recv()
+            dim = orders[number][stage]
+            lane = piece.lane_part * piece.lanes
+            region = outs[piece.ref].at[piece.slices(held[number], bits, lane)]
+            copy = pltpu.make_async_remote_copy(
+                src_ref=region,
+                dst_ref=region,
+                send_sem=send_sems.at[number, stage],
+                recv_sem=recv_sems.at[number, stage],
+                device_id=partner(dim, coords, bits),
+                device_id_type=MESH,
+            )
+            copy.start()
+            held[number][dim] = None
+            last[number] = copy
+            sent.append(copy)
+    for number in range(len(pieces)):
+        last[number].wait_recv()
+    for copy in sent:
+        copy.wait_send()
+
+
+def gather_blocks(blocks, shapes, bits):
+    pieces = gather_pieces(shapes)
+    full = []
+    for (rows, lanes, wdim, parts), block in zip(shapes, blocks):
+        whole = Piece(0, rows, lanes, wdim, 0, False).shape(range(bits + 1))
+        full.append(jax.ShapeDtypeStruct(whole, block.dtype))
+    count = len(blocks)
+    return pl.pallas_call(
+        lambda *refs: gather_kernel(pieces, bits, count, *refs),
+        out_shape=full,
+        in_specs=[pl.BlockSpec(memory_space=pltpu.VMEM)] * count,
+        out_specs=[pl.BlockSpec(memory_space=pl.ANY)] * count,
+        scratch_shapes=[
+            pltpu.SemaphoreType.DMA((len(pieces), bits + 1)),
+            pltpu.SemaphoreType.DMA((len(pieces), bits + 1)),
+            pltpu.SemaphoreType.DMA((len(pieces),)),
+        ],
+        compiler_params=pltpu.CompilerParams(collective_id=0, has_side_effects=True),
+        name="gather_weights",
+    )(*blocks)
+
+
+def scatter_kernel(pieces, bits, count, *refs):
+    grads, outs = refs[:count], refs[count : 2 * count]
+    send_sems, recv_sems = refs[-2:]
+    slots = refs[2 * count : -2]
+    coords = coordinates(bits)
+    greet(coords, bits)
+    orders = [scatter_order(bits, piece.flipped) for piece in pieces]
+    left = [{dim: None for dim in range(bits + 1)} for _ in pieces]
+    current = [grads[piece.ref] for piece in pieces]
+    lanes_at = [piece.lane_part * piece.lanes for piece in pieces]
+    pending = [None] * len(pieces)
+    sent = []
+
+    def finish(number, stage):
+        copy, keep = pending[number]
+        copy.wait_recv()
+        slot = slots[number * (bits + 1) + stage]
+        mine = current[number][keep].astype(jnp.float32)
+        total = mine + slot[...].astype(jnp.float32)
+        current[number], lanes_at[number] = slot, 0
+        return slot, total
+
+    for stage in range(bits + 1):
+        for number, piece in enumerate(pieces):
+            if stage > 0:
+                slot, total = finish(number, stage - 1)
+                slot[...] = total.astype(slot.dtype)
+            dim = orders[number][stage]
+            picks = dict(left[number])
+            picks[dim] = 1 - coords[dim]
+            give = piece.slices(picks, bits, lanes_at[number])
+            picks[dim] = coords[dim]
+            keep = piece.slices(picks, bits, lanes_at[number])
+            copy = pltpu.make_async_remote_copy(
+                src_ref=current[number].at[give],
+                dst_ref=slots[number * (bits + 1) + stage],
+                send_sem=send_sems.at[number, stage],
+                recv_sem=recv_sems.at[number, stage],
+                device_id=partner(dim, coords, bits),
+                device_id_type=MESH,
+            )
+            copy.start()
+            del left[number][dim]
+            pending[number] = (copy, keep)
+            sent.append(copy)
+    for number, piece in enumerate(pieces):
+        slot, total = finish(number, bits)
+        lane = piece.lane_part * piece.lanes
+        outs[piece.ref][:, pl.ds(lane, piece.lanes)] = total
+    for copy in sent:
+        copy.wait_send()
+
+
+def scatter_blocks(grads, shapes, bits):
+    pieces = gather_pieces(shapes)
+    slots = []
+    for piece in pieces:
+        dims = list(range(bits + 1))
+        for dim in scatter_order(bits, piece.flipped):
+            dims.remove(dim)
+            slots.append(pltpu.VMEM(piece.shape(dims), grads[piece.ref].dtype))
+    count = len(grads)
+    return pl.pallas_call(
+        lambda *refs: scatter_kernel(pieces, bits, count, *refs),
+        out_shape=[
+            jax.ShapeDtypeStruct((rows, lanes), jnp.float32) for rows, lanes, _, _ in shapes
+        ],
+        in_specs=[pl.BlockSpec(memory_space=pltpu.VMEM)] * count,
+        out_specs=[pl.BlockSpec(memory_space=pltpu.VMEM)] * count,
+        scratch_shapes=slots
+        + [
+            pltpu.SemaphoreType.DMA((len(pieces), bits + 1)),
+            pltpu.SemaphoreType.DMA((len(pieces), bits + 1)),
+        ],
+        compiler_params=pltpu.CompilerParams(
+            collective_id=1, has_side_effects=True, vmem_limit_bytes=60 * 1024 * 1024
+        ),
+        name="scatter_grads",
+    )(*grads)
+
+
 def shards(block_input, attn_in, attn_out, ffn_in, ffn_out, norm_gains, head_gains, cotangent):
-    paired = (
-        lax.all_gather(attn_in, "wshard", axis=0, tiled=True),
-        lax.all_gather(attn_out, "wshard", axis=0, tiled=True),
-        lax.all_gather(ffn_in, "wshard", axis=0, tiled=True),
-        lax.all_gather(ffn_out, "wshard", axis=0, tiled=True),
-        lax.all_gather(norm_gains, "wshard", axis=0, tiled=True),
-        lax.all_gather(head_gains, "wshard", axis=0, tiled=True),
-    )
-    whole = (
-        lax.all_gather(paired[0], "seq", axis=1, tiled=True),
-        lax.all_gather(paired[1], "seq", axis=1, tiled=True),
-        lax.all_gather(paired[2], "seq", axis=1, tiled=True),
-        lax.all_gather(paired[3], "seq", axis=1, tiled=True),
-        lax.all_gather(paired[4], "seq", axis=1, tiled=True),
-        lax.all_gather(paired[5], "seq", axis=1, tiled=True),
-    )
-    whole_attnin, whole_attnout, whole_ffnin, whole_ffnout, whole_norms, whole_heads = whole
+    seq_count = lax.axis_size("seq")
+    bits = axis_bits(seq_count)
+    gain_rows, gain_cols = norm_gains.shape
+    head_rows, head_cols = head_gains.shape
+    width = block_input.shape[-1]
+    gain_block = jnp.concatenate(
+        [
+            jnp.pad(norm_gains, ((0, 0), (0, 128 - gain_cols))),
+            jnp.pad(head_gains, ((0, 16 - gain_rows - head_rows), (0, 128 - head_cols))),
+        ],
+        axis=0,
+    )
+    wide = ffn_in.shape[1] % 256 == 0
+    up_block = ffn_in if wide else ffn_in.T
+    in_block, out_block, down_block = (attn_in.T, attn_out.T, ffn_out.T)
+    layouts = (
+        (*in_block.shape, "lead", 1),
+        (*out_block.shape, "lanes", 1),
+        (*up_block.shape, "rows", 2) if wide else (*up_block.shape, "lead", 1),
+        (*down_block.shape, "lanes", 1),
+    )
+    gathered = gather_blocks(
+        (in_block, out_block, up_block, down_block, gain_block),
+        layouts + ((16, 128, "lead", 1),),
+        bits,
+    )
+    in_halves = gathered[0].reshape(2, -1, in_block.shape[1])
+    attnin_t = jnp.concatenate([in_halves[0], in_halves[1]], axis=1)
+    attnout_t = gathered[1].reshape(width, -1)
+    if wide:
+        whole_ffnin = (
+            gathered[2]
+            .reshape(seq_count, width, up_block.shape[1])
+            .transpose(1, 0, 2)
+            .reshape(width, -1)
+        )
+    else:
+        up_halves = gathered[2].reshape(2, -1, up_block.shape[1])
+        whole_ffnin = jnp.concatenate([up_halves[0], up_halves[1]], axis=1).T
+    ffnout_t = gathered[3].reshape(width, -1)
+    gain_all = gathered[4].reshape(2, seq_count, 16, 128)
+    whole_norms = (
+        gain_all[:, :, :gain_rows, :gain_cols].transpose(0, 2, 1, 3).reshape(2 * gain_rows, -1)
+    )
+    whole_heads = (
+        gain_all[:, :, gain_rows : gain_rows + head_rows, :head_cols]
+        .transpose(0, 2, 1, 3)
+        .reshape(2 * head_rows, -1)
+    )
     gain_table = whole_norms.astype(jnp.float32)
     head_table = whole_heads.astype(jnp.float32)
     tokens = block_input[0]
@@ -121,7 +391,7 @@
     positions = lax.axis_index("seq") * row_count + jnp.arange(row_count, dtype=jnp.int32)
     normed_in, unit_in, inverse_in = rms_forward(tokens, gain_table[0])
     hidden_in = normed_in.astype(jnp.bfloat16)
-    projected = jnp.dot(hidden_in, whole_attnin, preferred_element_type=jnp.float32)
+    projected = jnp.dot(hidden_in, attnin_t.T, preferred_element_type=jnp.float32)
     query_raw = projected[:, : NQ * HD].reshape(row_count, NQ, HD)
     key_raw = projected[:, NQ * HD : (NQ + 1) * HD].reshape(row_count, 1, HD)
     value_raw = projected[:, (NQ + 1) * HD :]
@@ -149,7 +419,7 @@
     allowed = window_mask(jnp.repeat(positions, NQ), key_positions)
     mixture, log_totals = attend(query_rot, keys_all, values_all, allowed)
     attended = mixture.reshape(row_count, NQ * HD)
-    attn_proj = jnp.dot(attended, whole_attnout, preferred_element_type=jnp.float32)
+    attn_proj = jnp.dot(attended, attnout_t.T, preferred_element_type=jnp.float32)
     post_attn, unit_attn, inverse_attn = rms_forward(attn_proj, gain_table[1])
     middle = tokens + post_attn
     normed_mid, unit_mid, inverse_mid = rms_forward(middle, gain_table[2])
@@ -157,13 +427,13 @@
     gate_up = jnp.dot(hidden_mid, whole_ffnin, preferred_element_type=jnp.float32)
     activated, gelu_back = jax.vjp(gated_gelu, gate_up[:, :FF], gate_up[:, FF:])
     activated_bf = activated.astype(jnp.bfloat16)
-    ffn_proj = jnp.dot(activated_bf, whole_ffnout, preferred_element_type=jnp.float32)
+    ffn_proj = jnp.dot(activated_bf, ffnout_t.T, preferred_element_type=jnp.float32)
     post_ffn, unit_ffn, inverse_ffn = rms_forward(ffn_proj, gain_table[3])
     output = middle + post_ffn
     d_ffnproj, gain_four = rms_backward(unit_ffn, inverse_ffn, gain_table[3], upstream_out)
     d_ffn_bf = d_ffnproj.astype(jnp.bfloat16)
-    grad_ffnout = jnp.dot(activated_bf.T, d_ffn_bf, preferred_element_type=jnp.float32)
-    d_activated = jnp.dot(d_ffn_bf, whole_ffnout.T, preferred_element_type=jnp.float32)
+    grad_ffnout = jnp.dot(d_ffn_bf.T, activated_bf, preferred_element_type=jnp.float32)
+    d_activated = jnp.dot(d_ffn_bf, ffnout_t, preferred_element_type=jnp.float32)
     d_gate, d_up = gelu_back(d_activated)
     d_gateup = jnp.concatenate([d_gate, d_up], axis=1).astype(jnp.bfloat16)
     grad_ffnin = jnp.dot(hidden_mid.T, d_gateup, preferred_element_type=jnp.float32)
@@ -172,8 +442,8 @@
     d_middle = upstream_out + d_middle_part
     d_attnproj, gain_two = rms_backward(unit_attn, inverse_attn, gain_table[1], d_middle)
     d_attn_bf = d_attnproj.astype(jnp.bfloat16)
-    grad_attnout = jnp.dot(attended.T, d_attn_bf, preferred_element_type=jnp.float32)
-    d_mixed = jnp.dot(d_attn_bf, whole_attnout.T, preferred_element_type=jnp.float32).astype(
+    grad_attnout = jnp.dot(d_attn_bf.T, attended, preferred_element_type=jnp.float32)
+    d_mixed = jnp.dot(d_attn_bf, attnout_t, preferred_element_type=jnp.float32).astype(
         jnp.bfloat16
     )
     d_mixed = d_mixed.reshape(row_count * NQ, HD)
@@ -200,8 +470,18 @@
         ],
         axis=1,
     ).astype(jnp.bfloat16)
-    grad_attnin = jnp.dot(hidden_in.T, d_projected, preferred_element_type=jnp.float32)
-    d_normin = jnp.dot(d_projected, whole_attnin.T, preferred_element_type=jnp.float32)
+    half_width = in_block.shape[1]
+    grad_attnin = jnp.stack(
+        [
+            jnp.dot(
+                d_projected.T,
+                hidden_in[:, half * half_width : (half + 1) * half_width],
+                preferred_element_type=jnp.float32,
+            )
+            for half in range(2)
+        ]
+    )
+    d_normin = jnp.dot(d_projected, attnin_t, preferred_element_type=jnp.float32)
     d_tokens_part, gain_one = rms_backward(unit_in, inverse_in, gain_table[0], d_normin)
     input_grad = d_middle + d_tokens_part
     grad_norms = jnp.stack(
@@ -215,43 +495,50 @@
     grad_heads = jnp.stack(
         [jnp.sum(gain_query.reshape(-1, HD), axis=0), jnp.sum(gain_key.reshape(-1, HD), axis=0)]
     )
-    partial_sums = (
-        lax.psum_scatter(grad_attnin, "seq", scatter_dimension=1, tiled=True),
-        lax.psum_scatter(grad_attnout, "seq", scatter_dimension=1, tiled=True),
-        lax.psum_scatter(grad_ffnin, "seq", scatter_dimension=1, tiled=True),
-        lax.psum_scatter(grad_ffnout, "seq", scatter_dimension=1, tiled=True),
-        lax.psum_scatter(grad_norms, "seq", scatter_dimension=1, tiled=True),
-        lax.psum_scatter(grad_heads, "seq", scatter_dimension=1, tiled=True),
-    )
-    reduced = (
-        lax.psum_scatter(
-            partial_sums[0].astype(jnp.bfloat16), "wshard", scatter_dimension=0, tiled=True
-        ).astype(jnp.float32),
-        lax.psum_scatter(
-            partial_sums[1].astype(jnp.bfloat16), "wshard", scatter_dimension=0, tiled=True
-        ).astype(jnp.float32),
-        lax.psum_scatter(
-            partial_sums[2].astype(jnp.bfloat16), "wshard", scatter_dimension=0, tiled=True
-        ).astype(jnp.float32),
-        lax.psum_scatter(
-            partial_sums[3].astype(jnp.bfloat16), "wshard", scatter_dimension=0, tiled=True
-        ).astype(jnp.float32),
-        lax.psum_scatter(
-            partial_sums[4].astype(jnp.bfloat16), "wshard", scatter_dimension=0, tiled=True
-        ).astype(jnp.float32),
-        lax.psum_scatter(
-            partial_sums[5].astype(jnp.bfloat16), "wshard", scatter_dimension=0, tiled=True
-        ).astype(jnp.float32),
+    bit_dims = (2,) * bits
+    gain_sums = jnp.concatenate(
+        [
+            jnp.pad(
+                grad_norms.reshape(2, gain_rows, seq_count, gain_cols).transpose(0, 2, 1, 3),
+                ((0, 0), (0, 0), (0, 0), (0, 128 - gain_cols)),
+            ),
+            jnp.pad(
+                grad_heads.reshape(2, head_rows, seq_count, head_cols).transpose(0, 2, 1, 3),
+                ((0, 0), (0, 0), (0, 8 - gain_rows - head_rows), (0, 128 - head_cols)),
+            ),
+        ],
+        axis=2,
+    )
+    up_sums = grad_ffnin.astype(jnp.bfloat16)
+    if wide:
+        up_sums = (
+            up_sums.reshape(width, seq_count, -1)
+            .transpose(1, 0, 2)
+            .reshape(bit_dims + (width, up_block.shape[1]))
+        )
+    else:
+        up_sums = up_sums.reshape(2, up_block.shape[1], -1).transpose(0, 2, 1)
+        up_sums = up_sums.reshape((2,) + bit_dims + up_block.shape)
+    reduced = scatter_blocks(
+        (
+            grad_attnin.astype(jnp.bfloat16).reshape((2,) + bit_dims + in_block.shape),
+            grad_attnout.astype(jnp.bfloat16).reshape(bit_dims + (out_block.shape[0], -1)),
+            up_sums,
+            grad_ffnout.astype(jnp.bfloat16).reshape(bit_dims + (down_block.shape[0], -1)),
+            gain_sums.reshape((2,) + bit_dims + (8, 128)),
+        ),
+        layouts + ((8, 128, "lead", 1),),
+        bits,
     )
     return (
         output[None],
         input_grad[None],
-        reduced[0],
-        reduced[1],
-        reduced[2],
-        reduced[3],
-        reduced[4],
-        reduced[5],
+        reduced[0].T,
+        reduced[1].T,
+        reduced[2] if wide else reduced[2].T,
+        reduced[3].T,
+        reduced[4][:gain_rows, :gain_cols],
+        reduced[4][gain_rows : gain_rows + head_rows, :head_cols],
     )
 
 

time: 678 us -> 282 us (0.42)
  waiting for transfers between devices: 427 us -> 0.02 us
  Pallas kernels: 0 us -> 169 us
  blocking collectives: 137 us -> 0 us
  local copies, waits for them, and re-layouts: 20.7 us -> 44.6 us
  between operations: 16.6 us -> 1.95 us
  other arithmetic: 24.6 us -> 16.7 us
  matrix products: 35 us -> 27.8 us
    reduce_scatter x7 -> x0, waiting for transfers between devices: 265 us -> none  [the longest x1 76.8 us: shards(): lax.psum_scatter(grad_ffnout, 'seq', scatter_dimension=1, tiled=True)]
    pallas_call x0 -> x2, Pallas kernels: none -> 169 us  [the longest x1 90.7 us: scatter_blocks(): pl.pallas_call(lambda *refs: scatter_kernel(pieces, bits, count, *refs),...]
    all_gather x4 -> x0, waiting for transfers between devices: 93.6 us -> none  [the longest x1 54.8 us: shards(): lax.all_gather(paired[2], 'seq', axis=1, tiled=True)]
    all_gather x8 -> x0, blocking collectives: 71.9 us -> none  [the longest x1 21.8 us: shards(): lax.all_gather(paired[4], 'seq', axis=1, tiled=True)]
    unnamed x15 -> x0, waiting for transfers between devices: 68.9 us -> none
    unnamed x2 -> x0, blocking collectives: 64.9 us -> none
    convert_element_type x11 -> x1, other arithmetic: 13.1 us -> 0.1 us  [shards(): hidden_in = normed_in.astype(jnp.bfloat16)]
    reshape x0 -> x3, local copies, waits for them, and re-layouts: none -> 10.8 us  [the longest x1 7.9 us: shards(): whole_ffnin = gathered[2].reshape(seq_count, width, up_block.shape[1]).tr...]
  transfers between devices with their start and end apart: 21 -> 8, of which waited for: 11 -> 0; matrix products, arithmetic and copies ran while one was open for 9% -> 8% of each run, Pallas kernels for 0% -> 0%
where the time goes in v1:
time: 282 us; the launch traced here: 281 us
  Pallas kernels  169 us (60%)
  local copies, waits for them, and re-layouts  44.6 us (16%)
  matrix products  27.8 us (10%)
  starting transfers between devices  20.3 us (7%)
  other arithmetic  16.7 us (6%)
    pallas_call x1, Pallas kernels, scatter_blocks(): pl.pallas_call(lambda *refs: scatter_kernel(pieces, bits, count, *refs),...  90.7 us
    pallas_call x1, Pallas kernels, gather_blocks(): pl.pallas_call(lambda *refs: gather_kernel(pieces, bits, count, *refs), o...  78.8 us
    ppermute x8, starting transfers between devices, shifted(): lax.ppermute(value, axis, [(source, source + steps) for source in range(i...  20.3 us
    unnamed x166, local copies, waits for them, and re-layouts  17.1 us
    reshape x1, local copies, waits for them, and re-layouts, shards(): whole_ffnin = gathered[2].reshape(seq_count, width, up_block.shape[1]).tr...  7.9 us
  transfers between devices with their start and end apart: 8, of which 0 were waited for; matrix products, arithmetic and copies ran while one was open for 8% of the time, Pallas kernels for 0%

profile of v1, /device:TPU:0, one launch (start us, length us, event | category | flops | bytes accessed | tf_op | source)
XLA Modules:
  0.0 280.9 jit_solution(14382266993937062431)
XLA Ops:
  1.9 78.8 %gather_weights.1 = (bf16[2,2,2,2,2,96,320]{6,5,4,3,2,1,0:T(8,128)(2,1)}, bf16[2,2,2,2,40,1024]{5,4,3,2,1,0:T(8,128)(2,1)}, bf16[2,2,2,2,640,256]{5,4,3,2,1,0:T(...) custom-call(bf16[96,320]{1,0:T(8,128)(2,1)} %bitcast.143, ...), custom_call_target="tpu_custom_call" | custom-call | tf_op jit(solution)/shard_map/gather_weights/pallas_call | solution.py:239
  83.7 2.0 fusion.71
  89.0 4.1 %collective-permute-start = (bf16[128,512]{1,0:T(8,128)(2,1)}, bf16[128,512]{1,0:T(8,128)(2,1)}, u32[]{:S(2)}, u32[]{:S(2)}) collective-permute-start(bf16[128,512]{1,0:T(8,128)(2,1)} %pad_maximum_fusion.10), channel_id=1, source_target_pairs={{0,8},{2,10},{4,12},{6,14},{8,16},{10,18},{12,20},{14,22},{16,24},... | collective-permute-start | bytes 393224 | tf_op jit(solution)/shard_map/ppermute | solution.py:23
  93.1 2.8 %collective-permute-start.1 = (bf16[128,512]{1,0:T(8,128)(2,1)}, bf16[128,512]{1,0:T(8,128)(2,1)}, u32[]{:S(2)}, u32[]{:S(2)}) collective-permute-start(bf16[128,512]{1,0:T(8,128)(2,1)} %pad_maximum_fusion.10), channel_id=1, source_target_pairs={{0,6},{2,8},{4,10},{6,12},{8,14},{10,16},{12,18},{14,20},{16,22},{... | collective-permute-start | bytes 393224 | tf_op jit(solution)/shard_map/ppermute | solution.py:23
  95.9 6.2 %collective-permute-start.2 = (bf16[128,512]{1,0:T(8,128)(2,1)}, bf16[128,512]{1,0:T(8,128)(2,1)}, u32[]{:S(2)}, u32[]{:S(2)}) collective-permute-start(bf16[128,512]{1,0:T(8,128)(2,1)} %pad_maximum_fusion.10), channel_id=1, source_target_pairs={{0,4},{2,6},{4,8},{6,10},{8,12},{10,14},{12,16},{14,18},{16,20},{1... | collective-permute-start | bytes 393224 | tf_op jit(solution)/shard_map/ppermute | solution.py:23
  102.1 1.9 collective-permute-start.3
  109.8 7.9 %copy.23 = bf16[16,640,256]{1,2,0:T(8,128)(2,1)} copy(bf16[16,640,256]{2,1,0:T(8,128)(2,1)} %bitcast.113) | data formatting | bytes 10485760 | tf_op jit(solution)/shard_map/reshape | solution.py:368
  128.7 4.2 %fusion.70 = f32[128,4096]{1,0:T(8,128)S(1)} fusion(bf16[640,4096]{0,1:T(8,128)(2,1)} %bitcast.108, f32[128,640]{1,0:T(8,128)S(1)} %get-tuple-element.46, f32[640]{0:T(1024)S(1)} %get-tuple-element.41, f32[128]{0:T(128)S(1)} %add_rsqrt_fusion.2), kind=kOutput, calls=%fused_computation.182 | convolution fusion | flops 671334400 | bytes 7670784 | tf_op jit(solution)/shard_map/dot_general | solution.py:427
  133.3 1.5 copy-done.8
  139.5 1.6 multiply_reduce_fusion.3
  146.3 2.2 fusion.15
  151.4 1.6 convolution_convert_fusion.4
  153.1 4.2 %convolution_convert_fusion = bf16[640,4096]{1,0:T(8,128)(2,1)} fusion(bf16[128,2048]{1,0:T(8,128)(2,1)S(1)} %copy-done.35, bf16[128,2048]{1,0:T(8,128)(2,1)S(1)} %copy-done.33, f32[128,640]{1,0:T(8,128)S(1)} %get-tuple-element.46, f32[640]{0:T(1024)S(1)} %get-tuple-element.41, f32[128]{0:T(128)S(1)} %copy-done.51), kind=kOutput, calls=%fused_computation | convolution fusion | flops 676052992 | bytes 6622208 | tf_op jit(solution)/shard_map/dot_general | solution.py:439
  157.3 2.4 convolution_convert_fusion.1
  160.5 1.4 collective-permute-start.7
  161.9 1.3 collective-permute-start.6
  163.2 1.3 collective-permute-start.5
  168.1 1.4 copy-done
  169.5 2.9 %copy.42 = bf16[80,16,8,256]{3,2,0,1:T(8,128)(2,1)} copy(bf16[80,16,8,256]{3,2,1,0:T(8,128)(2,1)S(1)} %bitcast.106) | data formatting | bytes 10485760 | tf_op jit(solution)/shard_map/reshape | solution.py:515
  177.3 1.5 convolution_convert_fusion.3
  179.5 1.7 copy.27
  181.4 1.9 pad_maximum_fusion.refs_0_
  184.0 90.7 %scatter_grads.1 = (f32[96,320]{1,0:T(8,128)}, f32[40,512]{1,0:T(8,128)}, f32[320,256]{1,0:T(8,128)}, f32[40,1024]{1,0:T(8,128)}, f32[8,128]{1,0:T(8,128)}) custom-call(bf16[2,2,2,2,2,96,320]{6,5,4,3,2,1,0:T(8,128)(2,1)} %pad_maximum_fusion.refs_0_, bf16[2,2,2,2,40,1024]{5,4,3,2,1,0:T(8,128)(2,1)} %bitcast.116, bf16[2,2,2,2,640,256]{5,4,3,2,1,0:T(8,128)(2,1)} %bitcast.107, ...), custom_call_target="tpu_custom_call" | custom-call | tf_op jit(solution)/shard_map/scatter_grads/pallas_call | solution.py:316
  274.8 1.3 slice.162
  (271 shorter events, 52.0 us)
Async XLA Ops:
  87.2 17.8 %copy-start.56 = (f32[128]{0:T(128)}, f32[128]{0:T(128)S(1)}, u32[]{:S(2)}) copy-start(f32[128]{0:T(128)S(1)} %multiply_exponential_fusion) | copy-start | bytes 1540
  87.3 17.8 %copy-start.60 = (f32[128]{0:T(128)}, f32[128]{0:T(128)S(1)}, u32[]{:S(2)}) copy-start(f32[128]{0:T(128)S(1)} %get-tuple-element.79) | copy-start | bytes 1540
  89.0 30.4 %collective-permute-start = (bf16[128,512]{1,0:T(8,128)(2,1)}, bf16[128,512]{1,0:T(8,128)(2,1)}, u32[]{:S(2)}, u32[]{:S(2)}) collective-permute-start(bf16[128,512]{1,0:T(8,128)(2,1)} %pad_maximum_fusion.10), channel_id=1, source_target_pairs={{0,8},{2,10},{4,12},{6,14},{8,16},{10,18},{12,20},{14,22},{16,24},... | collective-permute-start | bytes 393224 | tf_op jit(solution)/shard_map/ppermute | solution.py:23
  93.1 27.2 %collective-permute-start.1 = (bf16[128,512]{1,0:T(8,128)(2,1)}, bf16[128,512]{1,0:T(8,128)(2,1)}, u32[]{:S(2)}, u32[]{:S(2)}) collective-permute-start(bf16[128,512]{1,0:T(8,128)(2,1)} %pad_maximum_fusion.10), channel_id=1, source_target_pairs={{0,6},{2,8},{4,10},{6,12},{8,14},{10,16},{12,18},{14,20},{16,22},{... | collective-permute-start | bytes 393224 | tf_op jit(solution)/shard_map/ppermute | solution.py:23
  95.9 25.3 %collective-permute-start.2 = (bf16[128,512]{1,0:T(8,128)(2,1)}, bf16[128,512]{1,0:T(8,128)(2,1)}, u32[]{:S(2)}, u32[]{:S(2)}) collective-permute-start(bf16[128,512]{1,0:T(8,128)(2,1)} %pad_maximum_fusion.10), channel_id=1, source_target_pairs={{0,4},{2,6},{4,8},{6,10},{8,12},{10,14},{12,16},{14,18},{16,20},{1... | collective-permute-start | bytes 393224 | tf_op jit(solution)/shard_map/ppermute | solution.py:23
  102.1 20.1 %collective-permute-start.3 = (bf16[128,512]{1,0:T(8,128)(2,1)}, bf16[128,512]{1,0:T(8,128)(2,1)}, u32[]{:S(2)}, u32[]{:S(2)}) collective-permute-start(bf16[128,512]{1,0:T(8,128)(2,1)} %pad_maximum_fusion.10), channel_id=1, source_target_pairs={{0,2},{2,4},{4,6},{6,8},{8,10},{10,12},{12,14},{14,16},{16,18},{18... | collective-permute-start | bytes 393224 | tf_op jit(solution)/shard_map/ppermute | solution.py:23
  107.0 10.7 %copy-start.13 = (f32[128,4]{1,0:T(8,128)}, f32[128,4]{1,0:T(8,128)S(1)}, u32[]{:S(2)}) copy-start(f32[128,4]{1,0:T(8,128)S(1)} %add_rsqrt_fusion) | copy-start | bytes 6148
  108.0 15.1 %copy-start.21 = (f32[128,4,128]{2,1,0:T(4,128)}, f32[128,4,128]{2,1,0:T(4,128)S(1)}, u32[]{:S(2)}) copy-start(f32[128,4,128]{2,1,0:T(4,128)S(1)} %get-tuple-element.57) | copy-start | bytes 786436
  108.0 15.1 %copy-start.23 = (f32[128,4,128]{2,1,0:T(4,128)}, f32[128,4,128]{2,1,0:T(4,128)S(1)}, u32[]{:S(2)}) copy-start(f32[128,4,128]{2,1,0:T(4,128)S(1)} %get-tuple-element.58) | copy-start | bytes 786436
  108.1 16.5 %copy-start.62 = (s32[640]{0:T(1024)}, s32[640]{0:T(1024)S(1)}, u32[]{:S(2)}) copy-start(s32[640]{0:T(1024)S(1)} %iota_add_fusion) | copy-start | bytes 7684
  108.1 16.4 %copy-start.70 = (pred[640]{0:T(1024)(128)(4,1)}, pred[640]{0:T(1024)(128)(4,1)S(1)}, u32[]{:S(2)}) copy-start(pred[640]{0:T(1024)(128)(4,1)S(1)} %broadcast_compare_fusion) | copy-start | bytes 1924
  117.9 5.3 %copy-start.54 = (s32[512]{0:T(512)S(1)}, s32[512]{0:T(512)}, u32[]{:S(2)}) copy-start(s32[512]{0:T(512)} %copy-done.53) | copy-start | bytes 6148
  128.7 12.4 %copy-start.50 = (f32[128]{0:T(128)}, f32[128]{0:T(128)S(1)}, u32[]{:S(2)}) copy-start(f32[128]{0:T(128)S(1)} %add_rsqrt_fusion.2) | copy-start | bytes 1540
  148.5 11.1 %copy-start.9 = (f32[640,256]{1,0:T(8,128)}, f32[640,256]{1,0:T(8,128)S(1)}, u32[]{:S(2)}) copy-start(f32[640,256]{1,0:T(8,128)S(1)} %fusion.15) | copy-start | bytes 1966084
  159.7 7.3 %copy-start.31 = (f32[128,128]{1,0:T(8,128)S(1)}, f32[128,128]{1,0:T(8,128)}, u32[]{:S(2)}) copy-start(f32[128,128]{1,0:T(8,128)} %copy-done.30) | copy-start | bytes 196612
  159.7 7.3 %copy-start.39 = (f32[128,128]{1,0:T(8,128)S(1)}, f32[128,128]{1,0:T(8,128)}, u32[]{:S(2)}) copy-start(f32[128,128]{1,0:T(8,128)} %get-tuple-element.67) | copy-start | bytes 196612
  160.5 6.7 %copy-start.14 = (f32[128,4]{1,0:T(8,128)S(1)}, f32[128,4]{1,0:T(8,128)}, u32[]{:S(2)}) copy-start(f32[128,4]{1,0:T(8,128)} %copy-done.13) | copy-start | bytes 6148
  160.5 6.7 %copy-start.46 = (f32[256]{0:T(256)S(1)}, f32[256]{0:T(256)}, u32[]{:S(2)}) copy-start(f32[256]{0:T(256)} %copy-done.45) | copy-start | bytes 3076
  160.5 13.2 %collective-permute-start.7 = (bf16[128,512]{1,0:T(8,128)(2,1)}, bf16[128,512]{1,0:T(8,128)(2,1)S(1)}, u32[]{:S(2)}, u32[]{:S(2)}) collective-permute-start(bf16[128,512]{1,0:T(8,128)(2,1)} %get-tuple-element.54), channel_id=1, source_target_pairs={{8,0},{10,2},{12,4},{14,6},{16,8},{18,10},{20,12},{22,14},{24,16},... | collective-permute-start | bytes 393224 | tf_op jit(solution)/shard_map/ppermute | solution.py:23
  161.9 11.8 %collective-permute-start.6 = (bf16[128,512]{1,0:T(8,128)(2,1)}, bf16[128,512]{1,0:T(8,128)(2,1)}, u32[]{:S(2)}, u32[]{:S(2)}) collective-permute-start(bf16[128,512]{1,0:T(8,128)(2,1)} %get-tuple-element.55), channel_id=1, source_target_pairs={{6,0},{8,2},{10,4},{12,6},{14,8},{16,10},{18,12},{20,14},{22,16},{... | collective-permute-start | bytes 393224 | tf_op jit(solution)/shard_map/ppermute | solution.py:23
  163.2 10.5 %collective-permute-start.5 = (bf16[128,512]{1,0:T(8,128)(2,1)}, bf16[128,512]{1,0:T(8,128)(2,1)}, u32[]{:S(2)}, u32[]{:S(2)}) collective-permute-start(bf16[128,512]{1,0:T(8,128)(2,1)} %get-tuple-element.56), channel_id=1, source_target_pairs={{4,0},{6,2},{8,4},{10,6},{12,8},{14,10},{16,12},{18,14},{20,16},{2... | collective-permute-start | bytes 393224 | tf_op jit(solution)/shard_map/ppermute | solution.py:23
  164.5 9.3 %collective-permute-start.4 = (bf16[128,512]{1,0:T(8,128)(2,1)}, bf16[128,512]{1,0:T(8,128)(2,1)}, u32[]{:S(2)}, u32[]{:S(2)}) collective-permute-start(bf16[128,512]{1,0:T(8,128)(2,1)} %get-tuple-element.53), channel_id=1, source_target_pairs={{2,0},{4,2},{6,4},{8,6},{10,8},{12,10},{14,12},{16,14},{18,16},{20... | collective-permute-start | bytes 393224 | tf_op jit(solution)/shard_map/ppermute | solution.py:23
  184.0 93.3 %copy-start.7 = (f32[128,640]{1,0:T(8,128)S(1)}, f32[128,640]{1,0:T(8,128)}, u32[]{:S(2)}) copy-start(f32[128,640]{1,0:T(8,128)} %copy-done.6) | copy-start | bytes 983044
  274.8 5.4 %copy-start.40 = (f32[40,1024]{1,0:T(8,128)S(1)}, f32[40,1024]{1,0:T(8,128)}, u32[]{:S(2)}) copy-start(f32[40,1024]{1,0:T(8,128)} %get-tuple-element.26) | copy-start | bytes 491524
  (60 other events, 126.4 us)

commit v2 on v1

--- a/solution.py
+++ b/solution.py
@@ -133,22 +133,17 @@
 
 
 class Piece:
-    def __init__(self, ref, rows, lanes, wdim, lane_part, flipped, dtype=jnp.bfloat16):
+    def __init__(self, ref, rows, lanes, wdim, row_part, flipped, dtype=jnp.bfloat16):
         self.ref, self.rows, self.lanes, self.wdim = ref, rows, lanes, wdim
-        self.lane_part, self.flipped, self.dtype = lane_part, flipped, dtype
-
-    def slices(self, picks, bits, base_lane):
+        self.row_part, self.flipped, self.dtype = row_part, flipped, dtype
+
+    def slices(self, picks, bits, base_row):
         index = []
-        rows, lanes = pl.ds(0, self.rows), pl.ds(base_lane, self.lanes)
+        rows, lanes = pl.ds(base_row, self.rows), pl.ds(0, self.lanes)
         if 0 in picks:
             pick = picks[0]
             if self.wdim == "lead":
                 index.append(slice(None) if pick is None else pick)
-            elif self.wdim == "rows":
-                if pick is None:
-                    rows = pl.ds(0, 2 * self.rows)
-                else:
-                    rows = pl.ds(pl.multiple_of(pick * self.rows, self.rows), self.rows)
             else:
                 if pick is None:
                     lanes = pl.ds(0, 2 * self.lanes)
@@ -165,21 +160,40 @@
         for dim in sorted(dims):
             if dim > 0 or self.wdim == "lead":
                 lead.append(2)
-            elif self.wdim == "rows":
-                rows *= 2
             else:
                 lanes *= 2
         return tuple(lead) + (rows, lanes)
 
 
-def gather_pieces(shapes):
-    out = []
+def make_pieces(shapes):
+    out, load = [], [0, 0]
     for number, (rows, lanes, wdim, parts) in enumerate(shapes):
+        if rows % (16 * parts):
+            parts = 1
         for part in range(parts):
-            out.append(
-                Piece(number, rows, lanes // parts, wdim, part, (part == 1) or (number % 2 == 1))
-            )
+            flipped = load[1] < load[0]
+            load[flipped] += rows * lanes // parts
+            out.append(Piece(number, rows // parts, lanes, wdim, part, flipped))
     return out
+
+
+def issue_order(pieces, orders, bits, shrinking):
+    free, ready, done = {}, [0.0] * len(pieces), [0] * len(pieces)
+    sequence = []
+    while len(sequence) < len(pieces) * (bits + 1):
+        number = min(
+            (n for n in range(len(pieces)) if done[n] <= bits), key=lambda n: (ready[n], done[n], n)
+        )
+        stage = done[number]
+        dim = orders[number][stage]
+        blocks = 2 ** (bits - stage) if shrinking else 2**stage
+        cost = 0.125 if dim == bits else (2.0 if 0 < dim < bits - 2 else 1.0)
+        start = max(ready[number], free.get(dim, 0.0))
+        finish = start + blocks * pieces[number].rows * pieces[number].lanes * cost
+        free[dim] = ready[number] = finish
+        done[number] += 1
+        sequence.append((number, stage))
+    return sequence
 
 
 def gather_kernel(pieces, bits, count, *refs):
@@ -189,10 +203,10 @@
     own = {dim: coords[dim] for dim in range(bits + 1)}
     local = []
     for number, piece in enumerate(pieces):
-        lane = piece.lane_part * piece.lanes
+        row = piece.row_part * piece.rows
         copy = pltpu.make_async_copy(
-            blocks[piece.ref].at[:, pl.ds(lane, piece.lanes)],
-            outs[piece.ref].at[piece.slices(own, bits, lane)],
+            blocks[piece.ref].at[pl.ds(row, piece.rows), :],
+            outs[piece.ref].at[piece.slices(own, bits, row)],
             local_sems.at[number],
         )
         copy.start()
@@ -202,27 +216,27 @@
     held = [dict(own) for _ in pieces]
     last = list(local)
     sent = []
-    for stage in range(bits + 1):
-        for number, piece in enumerate(pieces):
-            if stage == 0:
-                last[number].wait()
-            else:
-                last[number].wait_recv()
-            dim = orders[number][stage]
-            lane = piece.lane_part * piece.lanes
-            region = outs[piece.ref].at[piece.slices(held[number], bits, lane)]
-            copy = pltpu.make_async_remote_copy(
-                src_ref=region,
-                dst_ref=region,
-                send_sem=send_sems.at[number, stage],
-                recv_sem=recv_sems.at[number, stage],
-                device_id=partner(dim, coords, bits),
-                device_id_type=MESH,
-            )
-            copy.start()
-            held[number][dim] = None
-            last[number] = copy
-            sent.append(copy)
+    for number, stage in issue_order(pieces, orders, bits, False):
+        piece = pieces[number]
+        if stage == 0:
+            last[number].wait()
+        else:
+            last[number].wait_recv()
+        dim = orders[number][stage]
+        row = piece.row_part * piece.rows
+        region = outs[piece.ref].at[piece.slices(held[number], bits, row)]
+        copy = pltpu.make_async_remote_copy(
+            src_ref=region,
+            dst_ref=region,
+            send_sem=send_sems.at[number, stage],
+            recv_sem=recv_sems.at[number, stage],
+            device_id=partner(dim, coords, bits),
+            device_id_type=MESH,
+        )
+        copy.start()
+        held[number][dim] = None
+        last[number] = copy
+        sent.append(copy)
     for number in range(len(pieces)):
         last[number].wait_recv()
     for copy in sent:
@@ -230,7 +244,7 @@
 
 
 def gather_blocks(blocks, shapes, bits):
-    pieces = gather_pieces(shapes)
+    pieces = make_pieces(shapes)
     full = []
     for (rows, lanes, wdim, parts), block in zip(shapes, blocks):
         whole = Piece(0, rows, lanes, wdim, 0, False).shape(range(bits + 1))
@@ -260,52 +274,52 @@
     orders = [scatter_order(bits, piece.flipped) for piece in pieces]
     left = [{dim: None for dim in range(bits + 1)} for _ in pieces]
     current = [grads[piece.ref] for piece in pieces]
-    lanes_at = [piece.lane_part * piece.lanes for piece in pieces]
+    rows_at = [piece.row_part * piece.rows for piece in pieces]
     pending = [None] * len(pieces)
     sent = []
 
-    def finish(number, stage):
+    def finish(number, stage, kind):
         copy, keep = pending[number]
         copy.wait_recv()
         slot = slots[number * (bits + 1) + stage]
-        mine = current[number][keep].astype(jnp.float32)
-        total = mine + slot[...].astype(jnp.float32)
-        current[number], lanes_at[number] = slot, 0
+        mine = current[number][keep].astype(kind)
+        total = mine + slot[...].astype(kind)
+        current[number], rows_at[number] = slot, 0
         return slot, total
 
-    for stage in range(bits + 1):
-        for number, piece in enumerate(pieces):
-            if stage > 0:
-                slot, total = finish(number, stage - 1)
-                slot[...] = total.astype(slot.dtype)
-            dim = orders[number][stage]
-            picks = dict(left[number])
-            picks[dim] = 1 - coords[dim]
-            give = piece.slices(picks, bits, lanes_at[number])
-            picks[dim] = coords[dim]
-            keep = piece.slices(picks, bits, lanes_at[number])
-            copy = pltpu.make_async_remote_copy(
-                src_ref=current[number].at[give],
-                dst_ref=slots[number * (bits + 1) + stage],
-                send_sem=send_sems.at[number, stage],
-                recv_sem=recv_sems.at[number, stage],
-                device_id=partner(dim, coords, bits),
-                device_id_type=MESH,
-            )
-            copy.start()
-            del left[number][dim]
-            pending[number] = (copy, keep)
-            sent.append(copy)
+    for number, stage in issue_order(pieces, orders, bits, True):
+        piece = pieces[number]
+        if stage > 0:
+            slot, total = finish(number, stage - 1, current[number].dtype)
+            slot[...] = total.astype(slot.dtype)
+        dim = orders[number][stage]
+        picks = dict(left[number])
+        picks[dim] = 1 - coords[dim]
+        give = piece.slices(picks, bits, rows_at[number])
+        picks[dim] = coords[dim]
+        keep = piece.slices(picks, bits, rows_at[number])
+        copy = pltpu.make_async_remote_copy(
+            src_ref=current[number].at[give],
+            dst_ref=slots[number * (bits + 1) + stage],
+            send_sem=send_sems.at[number, stage],
+            recv_sem=recv_sems.at[number, stage],
+            device_id=partner(dim, coords, bits),
+            device_id_type=MESH,
+        )
+        copy.start()
+        del left[number][dim]
+        pending[number] = (copy, keep)
+        sent.append(copy)
     for number, piece in enumerate(pieces):
-        slot, total = finish(number, bits)
-        lane = piece.lane_part * piece.lanes
-        outs[piece.ref][:, pl.ds(lane, piece.lanes)] = total
+        slot, total = finish(number, bits, jnp.float32)
+        row = piece.row_part * piece.rows
+        outs[piece.ref][pl.ds(row, piece.rows), :] = total
     for copy in sent:
         copy.wait_send()
 
 
 def scatter_blocks(grads, shapes, bits):
-    pieces = gather_pieces(shapes)
+    pieces = make_pieces(shapes)
     slots = []
     for piece in pieces:
         dims = list(range(bits + 1))
@@ -349,9 +363,9 @@
     up_block = ffn_in if wide else ffn_in.T
     in_block, out_block, down_block = (attn_in.T, attn_out.T, ffn_out.T)
     layouts = (
-        (*in_block.shape, "lead", 1),
+        (*in_block.shape, "lead", 2),
         (*out_block.shape, "lanes", 1),
-        (*up_block.shape, "rows", 2) if wide else (*up_block.shape, "lead", 1),
+        (*up_block.shape, "lead", 4),
         (*down_block.shape, "lanes", 1),
     )
     gathered = gather_blocks(
@@ -365,8 +379,8 @@
     if wide:
         whole_ffnin = (
             gathered[2]
-            .reshape(seq_count, width, up_block.shape[1])
-            .transpose(1, 0, 2)
+            .reshape(2, seq_count, up_block.shape[0], up_block.shape[1])
+            .transpose(0, 2, 1, 3)
             .reshape(width, -1)
         )
     else:
@@ -512,9 +526,9 @@
     up_sums = grad_ffnin.astype(jnp.bfloat16)
     if wide:
         up_sums = (
-            up_sums.reshape(width, seq_count, -1)
-            .transpose(1, 0, 2)
-            .reshape(bit_dims + (width, up_block.shape[1]))
+            up_sums.reshape(2, up_block.shape[0], seq_count, -1)
+            .transpose(0, 2, 1, 3)
+            .reshape((2,) + bit_dims + up_block.shape)
         )
     else:
         up_sums = up_sums.reshape(2, up_block.shape[1], -1).transpose(0, 2, 1)

time: 282 us -> 271 us (0.961)
  Pallas kernels: 169 us -> 155 us
  local copies, waits for them, and re-layouts: 44.6 us -> 51 us
  starting transfers between devices: 20.3 us -> 17 us
    pallas_call x1, Pallas kernels: 90.7 us -> 79.6 us  [scatter_blocks(): pl.pallas_call(lambda *refs: scatter_kernel(pieces, bits, count, *refs),...]
    unnamed x166 -> x168, local copies, waits for them, and re-layouts: 17.1 us -> 24.5 us
    ppermute x8, starting transfers between devices: 20.3 us -> 17 us  [shifted(): lax.ppermute(value, axis, [(source, source + steps) for source in range(i...]
    pallas_call x1, Pallas kernels: 78.8 us -> 75.8 us  [gather_blocks(): pl.pallas_call(lambda *refs: gather_kernel(pieces, bits, count, *refs), o...]
  transfers between devices with their start and end apart: 8 -> 8, of which waited for: 0 -> 0; matrix products, arithmetic and copies ran while one was open for 8% -> 11% of each run, Pallas kernels for 0% -> 0%
where the time goes in v2:
time: 271 us; the launch traced here: 270 us
  Pallas kernels  155 us (57%)
  local copies, waits for them, and re-layouts  51 us (19%)
  matrix products  27.6 us (10%)
  starting transfers between devices  17 us (6%)
  other arithmetic  16.9 us (6%)
    pallas_call x1, Pallas kernels, scatter_blocks(): pl.pallas_call(lambda *refs: scatter_kernel(pieces, bits, count, *refs),...  79.6 us
    pallas_call x1, Pallas kernels, gather_blocks(): pl.pallas_call(lambda *refs: gather_kernel(pieces, bits, count, *refs), o...  75.8 us
    unnamed x168, local copies, waits for them, and re-layouts  24.5 us
    ppermute x8, starting transfers between devices, shifted(): lax.ppermute(value, axis, [(source, source + steps) for source in range(i...  17 us
    reshape x1, local copies, waits for them, and re-layouts, shards(): whole_ffnin = gathered[2].reshape(2, seq_count, up_block.shape[0], up_blo...  5.46 us
  transfers between devices with their start and end apart: 8, of which 0 were waited for; matrix products, arithmetic and copies ran while one was open for 11% of the time, Pallas kernels for 0%

profile of v2, /device:TPU:0, one launch (start us, length us, event | category | flops | bytes accessed | tf_op | source)
XLA Modules:
  0.0 270.0 jit_solution(17775893043734779899)
XLA Ops:
  1.9 75.8 %gather_weights.1 = (bf16[2,2,2,2,2,96,320]{6,5,4,3,2,1,0:T(8,128)(2,1)}, bf16[2,2,2,2,40,1024]{5,4,3,2,1,0:T(8,128)(2,1)}, bf16[2,2,2,2,2,320,256]{6,5,4,3,2,1,...) custom-call(bf16[96,320]{1,0:T(8,128)(2,1)} %bitcast.145, ...), custom_call_target="tpu_custom_call" | custom-call | tf_op jit(solution)/shard_map/gather_weights/pallas_call | solution.py:253
  80.7 2.0 fusion.71
  86.0 1.9 collective-permute-start
  87.9 4.4 %collective-permute-start.1 = (bf16[128,512]{1,0:T(8,128)(2,1)}, bf16[128,512]{1,0:T(8,128)(2,1)}, u32[]{:S(2)}, u32[]{:S(2)}) collective-permute-start(bf16[128,512]{1,0:T(8,128)(2,1)} %pad_maximum_fusion.10), channel_id=1, source_target_pairs={{0,6},{2,8},{4,10},{6,12},{8,14},{10,16},{12,18},{14,20},{16,22},{... | collective-permute-start | bytes 393224 | tf_op jit(solution)/shard_map/ppermute | solution.py:23
  92.3 3.1 %collective-permute-start.2 = (bf16[128,512]{1,0:T(8,128)(2,1)}, bf16[128,512]{1,0:T(8,128)(2,1)}, u32[]{:S(2)}, u32[]{:S(2)}) collective-permute-start(bf16[128,512]{1,0:T(8,128)(2,1)} %pad_maximum_fusion.10), channel_id=1, source_target_pairs={{0,4},{2,6},{4,8},{6,10},{8,12},{10,14},{12,16},{14,18},{16,20},{1... | collective-permute-start | bytes 393224 | tf_op jit(solution)/shard_map/ppermute | solution.py:23
  95.5 2.0 collective-permute-start.3
  103.1 5.5 %copy.23 = bf16[2,16,320,256]{3,1,2,0:T(8,128)(2,1)S(1)} copy(bf16[2,16,320,256]{3,2,1,0:T(8,128)(2,1)} %bitcast.115) | data formatting | bytes 10485760 | tf_op jit(solution)/shard_map/reshape | solution.py:382
  108.6 5.8 %copy.35 = bf16[80,8,16,256]{3,1,2,0:T(8,128)(2,1)} copy(bf16[80,8,16,256]{3,2,1,0:T(8,128)(2,1)S(1)} %bitcast.112) | data formatting | bytes 10485760
  125.5 3.5 %fusion.70 = f32[128,4096]{1,0:T(8,128)S(1)} fusion(bf16[640,4096]{1,0:T(8,128)(2,1)} %bitcast.106, f32[128,640]{1,0:T(8,128)S(1)} %get-tuple-element.46, f32[640]{0:T(1024)S(1)} %get-tuple-element.41, f32[128]{0:T(128)S(1)} %add_rsqrt_fusion.2), kind=kOutput, calls=%fused_computation.181 | convolution fusion | flops 671334400 | bytes 7670784 | tf_op jit(solution)/shard_map/dot_general | solution.py:441
  129.6 1.3 copy-done.8
  135.6 2.4 multiply_reduce_fusion.3
  143.1 2.2 fusion.15
  148.3 1.6 convolution_convert_fusion.4
  149.9 4.0 %convolution_convert_fusion = bf16[640,4096]{1,0:T(8,128)(2,1)} fusion(bf16[128,2048]{1,0:T(8,128)(2,1)S(1)} %copy-done.35, bf16[128,2048]{1,0:T(8,128)(2,1)S(1)} %copy-done.33, f32[128,640]{1,0:T(8,128)S(1)} %get-tuple-element.46, f32[640]{0:T(1024)S(1)} %get-tuple-element.41, f32[128]{0:T(128)S(1)} %copy-done.51), kind=kOutput, calls=%fused_computation | convolution fusion | flops 676052992 | bytes 6622208 | tf_op jit(solution)/shard_map/dot_general | solution.py:453
  153.9 2.4 convolution_convert_fusion.1
  157.1 1.4 collective-permute-start.7
  161.1 1.6 collective-permute-start.4
  165.0 1.4 copy-done
  166.4 1.8 copy.40
  168.3 4.3 %copy.29 = bf16[2,320,16,256]{3,1,2,0:T(8,128)(2,1)} copy(bf16[2,320,16,256]{3,2,1,0:T(8,128)(2,1)S(1)} %bitcast.113) | data formatting | bytes 10485760 | tf_op jit(solution)/shard_map/reshape | solution.py:529
  177.5 1.5 convolution_convert_fusion.3
  179.7 1.7 copy.27
  181.6 1.9 pad_maximum_fusion.refs_0_
  184.3 79.6 %scatter_grads.1 = (f32[96,320]{1,0:T(8,128)}, f32[40,512]{1,0:T(8,128)}, f32[320,256]{1,0:T(8,128)}, f32[40,1024]{1,0:T(8,128)}, f32[8,128]{1,0:T(8,128)}) custom-call(bf16[2,2,2,2,2,96,320]{6,5,4,3,2,1,0:T(8,128)(2,1)} %pad_maximum_fusion.refs_0_, bf16[2,2,2,2,40,1024]{5,4,3,2,1,0:T(8,128)(2,1)} %bitcast.118, ...), custom_call_target="tpu_custom_call" | custom-call | tf_op jit(solution)/shard_map/scatter_grads/pallas_call | solution.py:330
  (273 shorter events, 54.9 us)
Async XLA Ops:
  84.2 14.2 %copy-start.56 = (f32[128]{0:T(128)}, f32[128]{0:T(128)S(1)}, u32[]{:S(2)}) copy-start(f32[128]{0:T(128)S(1)} %multiply_exponential_fusion) | copy-start | bytes 1540
  84.3 14.2 %copy-start.60 = (f32[128]{0:T(128)}, f32[128]{0:T(128)S(1)}, u32[]{:S(2)}) copy-start(f32[128]{0:T(128)S(1)} %get-tuple-element.79) | copy-start | bytes 1540
  86.0 30.2 %collective-permute-start = (bf16[128,512]{1,0:T(8,128)(2,1)}, bf16[128,512]{1,0:T(8,128)(2,1)}, u32[]{:S(2)}, u32[]{:S(2)}) collective-permute-start(bf16[128,512]{1,0:T(8,128)(2,1)} %pad_maximum_fusion.10), channel_id=1, source_target_pairs={{0,8},{2,10},{4,12},{6,14},{8,16},{10,18},{12,20},{14,22},{16,24},... | collective-permute-start | bytes 393224 | tf_op jit(solution)/shard_map/ppermute | solution.py:23
  87.9 29.1 %collective-permute-start.1 = (bf16[128,512]{1,0:T(8,128)(2,1)}, bf16[128,512]{1,0:T(8,128)(2,1)}, u32[]{:S(2)}, u32[]{:S(2)}) collective-permute-start(bf16[128,512]{1,0:T(8,128)(2,1)} %pad_maximum_fusion.10), channel_id=1, source_target_pairs={{0,6},{2,8},{4,10},{6,12},{8,14},{10,16},{12,18},{14,20},{16,22},{... | collective-permute-start | bytes 393224 | tf_op jit(solution)/shard_map/ppermute | solution.py:23
  92.3 25.6 %collective-permute-start.2 = (bf16[128,512]{1,0:T(8,128)(2,1)}, bf16[128,512]{1,0:T(8,128)(2,1)}, u32[]{:S(2)}, u32[]{:S(2)}) collective-permute-start(bf16[128,512]{1,0:T(8,128)(2,1)} %pad_maximum_fusion.10), channel_id=1, source_target_pairs={{0,4},{2,6},{4,8},{6,10},{8,12},{10,14},{12,16},{14,18},{16,20},{1... | collective-permute-start | bytes 393224 | tf_op jit(solution)/shard_map/ppermute | solution.py:23
  95.5 23.5 %collective-permute-start.3 = (bf16[128,512]{1,0:T(8,128)(2,1)}, bf16[128,512]{1,0:T(8,128)(2,1)}, u32[]{:S(2)}, u32[]{:S(2)}) collective-permute-start(bf16[128,512]{1,0:T(8,128)(2,1)} %pad_maximum_fusion.10), channel_id=1, source_target_pairs={{0,2},{2,4},{4,6},{6,8},{8,10},{10,12},{12,14},{14,16},{16,18},{18... | collective-permute-start | bytes 393224 | tf_op jit(solution)/shard_map/ppermute | solution.py:23
  100.4 14.0 %copy-start.13 = (f32[128,4]{1,0:T(8,128)}, f32[128,4]{1,0:T(8,128)S(1)}, u32[]{:S(2)}) copy-start(f32[128,4]{1,0:T(8,128)S(1)} %add_rsqrt_fusion) | copy-start | bytes 6148
  101.4 18.4 %copy-start.21 = (f32[128,4,128]{2,1,0:T(4,128)}, f32[128,4,128]{2,1,0:T(4,128)S(1)}, u32[]{:S(2)}) copy-start(f32[128,4,128]{2,1,0:T(4,128)S(1)} %get-tuple-element.57) | copy-start | bytes 786436
  101.4 18.4 %copy-start.23 = (f32[128,4,128]{2,1,0:T(4,128)}, f32[128,4,128]{2,1,0:T(4,128)S(1)}, u32[]{:S(2)}) copy-start(f32[128,4,128]{2,1,0:T(4,128)S(1)} %get-tuple-element.58) | copy-start | bytes 786436
  101.5 19.8 %copy-start.62 = (s32[640]{0:T(1024)}, s32[640]{0:T(1024)S(1)}, u32[]{:S(2)}) copy-start(s32[640]{0:T(1024)S(1)} %iota_add_fusion) | copy-start | bytes 7684
  101.5 19.8 %copy-start.70 = (pred[640]{0:T(1024)(128)(4,1)}, pred[640]{0:T(1024)(128)(4,1)S(1)}, u32[]{:S(2)}) copy-start(pred[640]{0:T(1024)(128)(4,1)S(1)} %broadcast_compare_fusion) | copy-start | bytes 1924
  114.6 5.3 %copy-start.54 = (s32[512]{0:T(512)S(1)}, s32[512]{0:T(512)}, u32[]{:S(2)}) copy-start(s32[512]{0:T(512)} %copy-done.53) | copy-start | bytes 6148
  125.5 12.4 %copy-start.50 = (f32[128]{0:T(128)}, f32[128]{0:T(128)S(1)}, u32[]{:S(2)}) copy-start(f32[128]{0:T(128)S(1)} %add_rsqrt_fusion.2) | copy-start | bytes 1540
  145.4 10.9 %copy-start.9 = (f32[640,256]{1,0:T(8,128)}, f32[640,256]{1,0:T(8,128)S(1)}, u32[]{:S(2)}) copy-start(f32[640,256]{1,0:T(8,128)S(1)} %fusion.15) | copy-start | bytes 1966084
  156.3 7.6 %copy-start.31 = (f32[128,128]{1,0:T(8,128)S(1)}, f32[128,128]{1,0:T(8,128)}, u32[]{:S(2)}) copy-start(f32[128,128]{1,0:T(8,128)} %copy-done.30) | copy-start | bytes 196612
  156.3 7.6 %copy-start.39 = (f32[128,128]{1,0:T(8,128)S(1)}, f32[128,128]{1,0:T(8,128)}, u32[]{:S(2)}) copy-start(f32[128,128]{1,0:T(8,128)} %get-tuple-element.67) | copy-start | bytes 196612
  157.1 7.0 %copy-start.14 = (f32[128,4]{1,0:T(8,128)S(1)}, f32[128,4]{1,0:T(8,128)}, u32[]{:S(2)}) copy-start(f32[128,4]{1,0:T(8,128)} %copy-done.13) | copy-start | bytes 6148
  157.1 7.0 %copy-start.46 = (f32[256]{0:T(256)S(1)}, f32[256]{0:T(256)}, u32[]{:S(2)}) copy-start(f32[256]{0:T(256)} %copy-done.45) | copy-start | bytes 3076
  157.1 16.8 %collective-permute-start.7 = (bf16[128,512]{1,0:T(8,128)(2,1)}, bf16[128,512]{1,0:T(8,128)(2,1)S(1)}, u32[]{:S(2)}, u32[]{:S(2)}) collective-permute-start(bf16[128,512]{1,0:T(8,128)(2,1)} %get-tuple-element.54), channel_id=1, source_target_pairs={{8,0},{10,2},{12,4},{14,6},{16,8},{18,10},{20,12},{22,14},{24,16},... | collective-permute-start | bytes 393224 | tf_op jit(solution)/shard_map/ppermute | solution.py:23
  158.5 15.4 %collective-permute-start.6 = (bf16[128,512]{1,0:T(8,128)(2,1)}, bf16[128,512]{1,0:T(8,128)(2,1)}, u32[]{:S(2)}, u32[]{:S(2)}) collective-permute-start(bf16[128,512]{1,0:T(8,128)(2,1)} %get-tuple-element.55), channel_id=1, source_target_pairs={{6,0},{8,2},{10,4},{12,6},{14,8},{16,10},{18,12},{20,14},{22,16},{... | collective-permute-start | bytes 393224 | tf_op jit(solution)/shard_map/ppermute | solution.py:23
  159.8 14.1 %collective-permute-start.5 = (bf16[128,512]{1,0:T(8,128)(2,1)}, bf16[128,512]{1,0:T(8,128)(2,1)}, u32[]{:S(2)}, u32[]{:S(2)}) collective-permute-start(bf16[128,512]{1,0:T(8,128)(2,1)} %get-tuple-element.56), channel_id=1, source_target_pairs={{4,0},{6,2},{8,4},{10,6},{12,8},{14,10},{16,12},{18,14},{20,16},{2... | collective-permute-start | bytes 393224 | tf_op jit(solution)/shard_map/ppermute | solution.py:23
  161.1 12.8 %collective-permute-start.4 = (bf16[128,512]{1,0:T(8,128)(2,1)}, bf16[128,512]{1,0:T(8,128)(2,1)}, u32[]{:S(2)}, u32[]{:S(2)}) collective-permute-start(bf16[128,512]{1,0:T(8,128)(2,1)} %get-tuple-element.53), channel_id=1, source_target_pairs={{2,0},{4,2},{6,4},{8,6},{10,8},{12,10},{14,12},{16,14},{18,16},{20... | collective-permute-start | bytes 393224 | tf_op jit(solution)/shard_map/ppermute | solution.py:23
  184.3 82.2 %copy-start.7 = (f32[128,640]{1,0:T(8,128)S(1)}, f32[128,640]{1,0:T(8,128)}, u32[]{:S(2)}) copy-start(f32[128,640]{1,0:T(8,128)} %copy-done.6) | copy-start | bytes 983044
  263.9 5.4 %copy-start.40 = (f32[40,1024]{1,0:T(8,128)S(1)}, f32[40,1024]{1,0:T(8,128)}, u32[]{:S(2)}) copy-start(f32[40,1024]{1,0:T(8,128)} %get-tuple-element.26) | copy-start | bytes 491524
  (60 other events, 133.4 us)
